TPU v7x, 512 devices: a whole 4x8x8 slice. The times are simulated.
512 devices in a mesh: depth: 4 (over x), row: 8 (over z_hi, core), col: 16 (over z_lo, y).
Axes of the slice: x: 4, y: 8, z: 8 (z_hi: 4, z_lo: 2; z = z_hi * 2 + z_lo), core: 2. Of those that a mesh axis runs over, the one named last changes fastest.
Arguments:
- tokens: bfloat16 [512, 6144], P(('depth', 'row'), 'col'), may hold values from -6 to 6
- grad_out: bfloat16 [512, 6144], P(('depth', 'row'), 'col'), may hold values from -6 to 6
- w_up: bfloat16 [6144, 24576], P(('col', 'depth'), 'row'), may hold values from -0.078125 to 0.078125
- w_down: bfloat16 [6144, 24576], P(('col', 'depth'), 'row'), may hold values from -0.0390625 to 0.0390625
Outputs:
- grad_in: bfloat16 [512, 6144], P(('depth', 'row'), 'col')
- grad_up: bfloat16 [6144, 24576], P(('col', 'depth'), 'row')
- grad_down: bfloat16 [6144, 24576], P(('col', 'depth'), 'row')
All inputs are finite; a program needn't handle non-finite values.
Results may differ from a plain program's by a relative error of at most 0.03.
Values may be sent and summed in bfloat16 or wider, within the bound.
No kernel may reach another device: no remote copies, remote signals or barrier semaphores. Data moves between devices by JAX's collectives and lax.ppermute only.
A program may use at most 64 MiB of HBM per device.

v0:
```python
import math

import jax
import jax.numpy as jnp
from jax import lax
from jax.sharding import PartitionSpec as P


def gelu_parts(hidden):
    coeff = math.sqrt(2.0 / math.pi)
    cube = hidden * hidden * hidden
    slope_in = jnp.tanh(coeff * (hidden + 0.044715 * cube))
    value = 0.5 * hidden * (1.0 + slope_in)
    slope = 0.5 * (1.0 + slope_in) + 0.5 * hidden * (1.0 - slope_in * slope_in) * coeff * (
        1.0 + 3.0 * 0.044715 * hidden * hidden
    )
    return (value, slope)


def body(tokens, grad_out, w_up, w_down):
    depth_pos = lax.axis_index("depth")
    up_block, down_block = (
        lax.all_gather(w_up, "depth", axis=0, tiled=True),
        lax.all_gather(w_down, "depth", axis=0, tiled=True),
    )
    x_rows, dy_rows = (
        lax.all_gather(tokens, ("depth", "row"), axis=0, tiled=True),
        lax.all_gather(grad_out, ("depth", "row"), axis=0, tiled=True),
    )
    own_count = x_rows.shape[0] // lax.axis_size("depth")
    own_start = depth_pos * own_count
    x_own = lax.dynamic_slice_in_dim(x_rows, own_start, own_count, 0)
    dy_own = lax.dynamic_slice_in_dim(dy_rows, own_start, own_count, 0)
    narrow = w_up.shape[0]
    dy_narrow = lax.dynamic_slice_in_dim(dy_rows, depth_pos * narrow, narrow, 1)
    pre_part = jnp.dot(x_rows, up_block, preferred_element_type=jnp.float32)
    grad_part = jnp.dot(dy_own, down_block, preferred_element_type=jnp.float32)
    hidden_pre, act_grad = (
        lax.psum(pre_part.astype(jnp.bfloat16), "col").astype(jnp.float32),
        lax.psum(grad_part.astype(jnp.bfloat16), "col").astype(jnp.float32),
    )
    act_value, slope = gelu_parts(hidden_pre)
    act_rows = act_value.astype(jnp.bfloat16)
    slope_own = lax.dynamic_slice_in_dim(slope, own_start, own_count, 0)
    hidden_grad = (act_grad * slope_own).astype(jnp.bfloat16)
    grad_up = lax.psum_scatter(
        lax.dot_general(
            x_own, hidden_grad, (((0,), (0,)), ((), ())), preferred_element_type=jnp.float32
        ).astype(jnp.bfloat16),
        "depth",
        scatter_dimension=0,
        tiled=True,
    )
    grad_in = lax.psum_scatter(
        lax.dot_general(
            hidden_grad, up_block, (((1,), (1,)), ((), ())), preferred_element_type=jnp.float32
        ).astype(jnp.bfloat16),
        "row",
        scatter_dimension=0,
        tiled=True,
    )
    grad_down = lax.dot_general(
        dy_narrow, act_rows, (((0,), (0,)), ((), ())), preferred_element_type=jnp.float32
    ).astype(jnp.bfloat16)
    return (grad_in, grad_up, grad_down)


def solution(mesh):
    placed = (
        P(("depth", "row"), "col"),
        P(("depth", "row"), "col"),
        P(("col", "depth"), "row"),
        P(("col", "depth"), "row"),
    )
    return jax.shard_map(
        body,
        mesh=mesh,
        in_specs=placed,
        out_specs=(
            P(("depth", "row"), "col"),
            P(("col", "depth"), "row"),
            P(("col", "depth"), "row"),
        ),
        check_vma=False,
    )
```

profile of v0, /device:TPU:1, one launch (start us, length us, event | category | flops | bytes accessed | tf_op | source)
XLA Modules:
  0.0 356.0 jit_solution(12280223903495737786)
XLA Ops:
  7.2 0.0 all-gather.5.cloned.1.call-start
  7.2 0.7 all-gather.5.cloned.1.call-update
  7.9 0.0 all-gather.3.cloned.1.call-start
  7.9 0.7 all-gather.3.cloned.1.call-update
  8.6 0.0 all-reduce.3.cloned.1.call-start
  8.7 53.1 %all_gather.14 = bf16[512,384]{1,0:T(8,128)(2,1)S(1)} all-gather(bf16[16,384]{1,0:T(8,128)(2,1)} %param.4), channel_id=1, replica_groups=mesh['depth'=4,'row'=8,'col'=16] {'depth','row'}, dimensions={0}, use_global_device_ids=true | all-gather | bytes 405504 | tf_op jit(solution)/shard_map/all_gather | solution.py:27
  61.8 0.0 copy-start.4
  61.8 40.9 %all_gather.12 = bf16[512,384]{1,0:T(8,128)(2,1)S(1)} all-gather(bf16[16,384]{1,0:T(8,128)(2,1)} %param.5), channel_id=1, replica_groups=mesh['depth'=4,'row'=8,'col'=16] {'depth','row'}, dimensions={0}, use_global_device_ids=true | all-gather | bytes 405504 | tf_op jit(solution)/shard_map/all_gather | solution.py:28
  102.7 0.0 all-gather.5.cloned.1.call-done
  102.7 5.1 %convolution_convert_fusion = bf16[512,3072]{1,0:T(8,128)(2,1)} fusion(bf16[512,384]{1,0:T(8,128)(2,1)S(1)} %all_gather.14, bf16[384,3072]{1,0:T(8,128)(2,1)} %all-gather.5.cloned.1.call-done), kind=kOutput, calls=%fused_computation.6 | convolution fusion | flops 1209532416 | bytes 5898240 | tf_op jit(solution)/shard_map/dot_general | solution.py:36
  107.8 0.0 copy-done.4
  107.8 0.0 all-gather.3.cloned.1.call-done
  107.8 3.2 convolution_convert_fusion.2
  111.0 0.0 all-reduce.3.cloned.1.call-update
  111.0 0.0 reduce-scatter.3.cloned.1.call-start
  111.1 145.0 %all-reduce.3.cloned.1.call-done = (bf16[512,3072]{1,0:T(8,128)(2,1)}, bf16[128,3072]{1,0:T(8,128)(2,1)}) async-done(((bf16[512,3072]{1,0:T(8,128)(2,1)}, bf16[128,3072]{1,0:T(8,128)(2,1)}), (bf16[512,3072]{1,0:T(8,128)(2,1)}, bf16[128,3072]{1,0:T(8,128)(2,1)})) %all-reduce.3.cloned.1.call-update) | async-done | bytes 3932176 | tf_op jit(solution)/shard_map/psum | solution.py:39
  256.1 0.0 copy-start
  256.1 2.8 convert_element_type.30
  258.9 0.0 copy-done
  258.9 0.0 copy-start.3
  258.9 2.6 fusion.3
  261.5 0.0 copy-done.3
  261.5 0.0 copy-start.2
  261.5 0.7 fusion.8
  262.2 0.0 copy-start.1
  262.3 0.9 copy-done.1
  263.1 0.0 copy-done.2
  263.2 1.5 convolution_convert_fusion.4
  264.6 0.0 reduce-scatter.3.cloned.1.call-update
  264.7 0.0 reduce-scatter.5.cloned.1.call-start
  264.7 3.4 convolution_convert_fusion.1
  268.1 0.0 reduce-scatter.5.cloned.1.call-update
  268.2 3.3 convolution_convert_fusion.3
  271.5 38.2 %reduce-scatter.3.cloned.1.call-done = bf16[16,384]{1,0:T(8,128)(2,1)} async-done(((bf16[128,384]{1,0:T(8,128)(2,1)}), bf16[16,384]{1,0:T(8,128)(2,1)}) %reduce-scatter.3.cloned.1.call-update) | async-done | bytes 12304 | tf_op jit(solution)/shard_map/reduce_scatter | solution.py:54
  309.7 39.8 %reduce-scatter.5.cloned.1.call-done = bf16[96,3072]{1,0:T(8,128)(2,1)} async-done(((bf16[384,3072]{1,0:T(8,128)(2,1)}), bf16[96,3072]{1,0:T(8,128)(2,1)}) %reduce-scatter.5.cloned.1.call-update) | async-done | bytes 589840 | tf_op jit(solution)/shard_map/reduce_scatter | solution.py:46
Async XLA Ops:
  7.2 95.5 %all-gather.5.cloned.1.call-start = ((), (), s32[]{:S(2)}) async-start(), calls=%async_computation.3 | async-start | bytes 2949120 | tf_op jit(solution)/shard_map/all_gather | solution.py:23
  7.9 99.9 %all-gather.3.cloned.1.call-start = ((), (), s32[]{:S(2)}) async-start(), calls=%async_computation.2 | async-start | bytes 2949120 | tf_op jit(solution)/shard_map/all_gather | solution.py:24
  8.6 247.4 %all-reduce.3.cloned.1.call-start = ((), (), s32[]{:S(2)}) async-start(), calls=%async_computation.6 | async-start | bytes 7864320 | tf_op jit(solution)/shard_map/psum | solution.py:39
  61.8 46.0 %copy-start.4 = (bf16[512,384]{1,0:T(8,128)(2,1)}, bf16[512,384]{1,0:T(8,128)(2,1)S(1)}, u32[]{:S(2)}) copy-start(bf16[512,384]{1,0:T(8,128)(2,1)S(1)} %all_gather.14) | copy-start | bytes 1179652
  111.0 198.7 %reduce-scatter.3.cloned.1.call-start = ((), (), s32[]{:S(2)}) async-start(), calls=%async_computation.4 | async-start | bytes 110592 | tf_op jit(solution)/shard_map/reduce_scatter | solution.py:54
  256.1 2.9 copy-start
  258.9 2.6 copy-start.3
  261.5 1.7 copy-start.2
  262.2 0.9 copy-start.1
  264.7 84.8 %reduce-scatter.5.cloned.1.call-start = ((), (), s32[]{:S(2)}) async-start(), calls=%async_computation.5 | async-start | bytes 2949120 | tf_op jit(solution)/shard_map/reduce_scatter | solution.py:46
Sparse Core Ops, SparseCore 0:
  10.1 44.9 all-gather.4
  57.2 38.4 all-gather.2
  111.1 144.8 all-reduce.2
  264.8 44.8 reduce-scatter.2
  312.9 36.4 reduce-scatter.4
where the time goes:
time: 356 us
  waiting for transfers between devices  224 us (63%)
  blocking collectives  94 us (26%)
  matrix products  16.5 us (5%)
  between operations  13.9 us (4%)
  other arithmetic  6.11 us (2%)
    psum x1, waiting for transfers between devices, body(): lax.psum(pre_part.astype(jnp.bfloat16), 'col').astype(jnp.float32)  145 us
    all_gather x1, blocking collectives, body(): lax.all_gather(tokens, ('depth', 'row'), axis=0, tiled=True)  53.1 us
    all_gather x1, blocking collectives, body(): lax.all_gather(grad_out, ('depth', 'row'), axis=0, tiled=True)  40.9 us
    reduce_scatter x1, waiting for transfers between devices, body(): lax.psum_scatter(lax.dot_general(x_own, hidden_grad, (((0,), (0,)), ((),...  39.8 us
    reduce_scatter x1, waiting for transfers between devices, body(): lax.psum_scatter(lax.dot_general(hidden_grad, up_block, (((1,), (1,)), ((...  38.2 us
  transfers between devices with their start and end apart: 5, of which 3 were waited for; matrix products, arithmetic and copies ran while one was open for 3% of the time, Pallas kernels for 0%

commit v1 on v0

v1 whole, which is shorter than its diff:
```python
import math

import jax
import jax.numpy as jnp
from jax import lax
from jax.sharding import Mesh, PartitionSpec as P

bf16, f32 = jnp.bfloat16, jnp.float32
ROW = ("zhi", "core")
COL = ("zlo", "y")


def gelu_parts(hidden):
    coeff = math.sqrt(2.0 / math.pi)
    cube = hidden * hidden * hidden
    slope_in = jnp.tanh(coeff * (hidden + 0.044715 * cube))
    value = 0.5 * hidden * (1.0 + slope_in)
    slope = 0.5 * (1.0 + slope_in) + 0.5 * hidden * (1.0 - slope_in * slope_in) * coeff * (
        1.0 + 3.0 * 0.044715 * hidden * hidden
    )
    return (value, slope)


def after(value, *others):
    return lax.optimization_barrier((value,) + others)[0]


def contract(left, right, left_at, right_at):
    return lax.dot_general(
        left, right, (((left_at,), (right_at,)), ((), ())), preferred_element_type=f32
    )


def body(tokens, grad_out, w_up, w_down):
    n_depth = lax.axis_size("depth")
    n_row = lax.axis_size("zhi") * lax.axis_size("core")
    n_y = lax.axis_size("y")
    depth_pos = lax.axis_index("depth")
    pair_pos = lax.axis_index("zlo")
    narrow, hidden = w_up.shape
    own_rows, feats = tokens.shape
    group = own_rows * n_row
    half = group // 2
    piece = half // n_y

    def from_ahead(array, j):
        return lax.ppermute(array, "depth", [(i, (i - j) % n_depth) for i in range(n_depth)])

    def to_ahead(array, j):
        return lax.ppermute(array, "depth", [(i, (i + j) % n_depth) for i in range(n_depth)])

    def swap(array):
        return lax.ppermute(array, "zlo", [(0, 1), (1, 0)])

    def exchange(array, axis):
        return lax.all_to_all(array, axis, 0, 0, tiled=True)

    def copies(array, count):
        return jnp.broadcast_to(array[None], (count,) + array.shape)

    def rolled(array, start, axis):
        return lax.dynamic_slice_in_dim(
            jnp.concatenate([array, array], axis), start, array.shape[axis], axis
        )

    def gather(array):
        return jnp.concatenate([array] + [from_ahead(array, j) for j in range(1, n_depth)], 0)

    def summed(got):
        return jnp.sum(got.astype(f32), axis=0)

    up_block = exchange(copies(w_up, n_depth), "depth").reshape(feats, hidden)
    both = lax.all_gather(jnp.stack([tokens, grad_out]), ROW, axis=0)
    x_rows = both[:, 0].reshape(group, feats)
    dy_rows = rolled(both[:, 1].reshape(group, feats), pair_pos * half, 0)
    x_rot = rolled(x_rows, depth_pos * narrow, 1)
    dy_rot = rolled(dy_rows, depth_pos * narrow, 1)
    down_block = lax.all_gather(after(w_down, both), "depth", axis=0, tiled=True)

    pre_part = contract(x_rows, up_block, 1, 0).astype(bf16)
    sent = pre_part.reshape(2 * n_y, piece, hidden)
    pre = summed(exchange(sent, COL))
    act_value, slope = gelu_parts(pre)
    act_near = exchange(copies(act_value.astype(bf16), n_y), "y").reshape(half, hidden)

    grad_part = contract(dy_rows, after(down_block, pre_part), 1, 0).astype(bf16)
    grad_other = swap(grad_part[half:])
    grad_pair = (grad_part[:half].astype(f32) + grad_other.astype(f32)).astype(bf16)
    grad_pair = after(grad_pair, act_near).reshape(n_y, piece, hidden)
    act = jnp.concatenate([act_near, swap(act_near)], 0)
    down_part = contract(dy_rows, act, 0, 0).astype(bf16)
    act_grad = summed(exchange(grad_pair, "y"))
    mine = (act_grad * slope).astype(bf16)
    hidden_grad = exchange(copies(mine, 2 * n_y), COL).reshape(group, hidden)

    def scatter(part):
        return [part[:narrow]] + [
            to_ahead(part[j * narrow : (j + 1) * narrow], j) for j in range(1, n_depth)
        ]

    def total(parts):
        acc = parts[0].astype(f32)
        for part in parts[1:]:
            acc = acc + part.astype(f32)
        return acc.astype(bf16)

    grad_down = lax.psum_scatter(down_part, "depth", scatter_dimension=0, tiled=True)
    up_terms = scatter(contract(x_rot, hidden_grad, 0, 0).astype(bf16))
    grad_in_part = contract(hidden_grad, up_block, 1, 1).astype(bf16)
    grad_in_part = after(grad_in_part, up_terms[1])
    got = exchange(grad_in_part.reshape(n_row, own_rows, feats), ROW)
    grad_in = summed(got).astype(bf16)
    grad_up = total(up_terms)
    return (grad_in, grad_up, grad_down)


def solution(mesh):
    shape = mesh.devices.shape
    fine = Mesh(
        mesh.devices.reshape(shape[0], shape[1] // 2, 2, 2, shape[2] // 2),
        ("depth", "zhi", "core", "zlo", "y"),
    )
    tokens_at = P(("depth",) + ROW, ("zlo", "y"))
    weights_at = P(("zlo", "y", "depth"), ROW)
    return jax.shard_map(
        body,
        mesh=fine,
        in_specs=(tokens_at, tokens_at, weights_at, weights_at),
        out_specs=(tokens_at, weights_at, weights_at),
        check_vma=False,
    )
```

time: 356 us -> 199 us (0.56)
  the two profiles are of different devices: /device:TPU:1 before, /device:TPU:4 now
where the time goes in v1:
time: 199 us; the launch traced here: 198 us
  waiting for transfers between devices  89.8 us (45%)
  starting transfers between devices  55.7 us (28%)
  blocking collectives  15.3 us (8%)
  between operations  14.2 us (7%)
  matrix products  9.29 us (5%)
  local copies, waits for them, and re-layouts  8.29 us (4%)
  other arithmetic  5.5 us (3%)
    all_to_all x6, waiting for transfers between devices, exchange(): return lax.all_to_all(array, axis, 0, 0, tiled=True)  61 us
    all_to_all x6, starting transfers between devices, exchange(): return lax.all_to_all(array, axis, 0, 0, tiled=True)  39.1 us
    ppermute x3, waiting for transfers between devices, to_ahead(): lax.ppermute(array, 'depth', [(i, (i + j) % n_depth) for i in range(n_dep...  17.8 us
    all_gather x1, blocking collectives, body(): both = lax.all_gather(jnp.stack([tokens, grad_out]), ROW, axis=0)  15.3 us
    ppermute x2, waiting for transfers between devices, swap(): return lax.ppermute(array, 'zlo', [(0, 1), (1, 0)])  10.8 us
    ppermute x3, starting transfers between devices, to_ahead(): lax.ppermute(array, 'depth', [(i, (i + j) % n_depth) for i in range(n_dep...  10.7 us
    dot_general x5, matrix products, contract(): lax.dot_general(left, right, (((left_at,), (right_at,)), ((), ())), prefe...  9.29 us
    ppermute x2, starting transfers between devices, swap(): return lax.ppermute(array, 'zlo', [(0, 1), (1, 0)])  5.83 us
  transfers between devices with their start and end apart: 13, of which 9 were waited for; matrix products, arithmetic and copies ran while one was open for 8% of the time, Pallas kernels for 0%

profile of v1, /device:TPU:4, one launch (start us, length us, event | category | flops | bytes accessed | tf_op | source)
XLA Modules:
  0.0 198.1 jit_solution(11095558360030619572)
XLA Ops:
  7.2 2.8 %broadcast_in_dim.6 = bf16[4,96,3072]{2,1,0:T(8,128)(2,1)} broadcast(bf16[96,3072]{1,0:T(8,128)(2,1)} %param.6), dimensions={1,2} | broadcast | bytes 2949120 | tf_op jit(solution)/shard_map/broadcast_in_dim | solution.py:59
  10.0 0.0 copy-start.7
  10.0 0.0 copy-start.8
  10.0 9.6 %all-to-all-start = ((bf16[4,96,3072]{2,1,0:T(8,128)(2,1)}), bf16[4,96,3072]{2,1,0:T(8,128)(2,1)S(1)}, u32[]{:S(2)}, u32[]{:S(2)}) async-start(bf16[4,96,3072]{2,1,0:T(8,128)(2,1)} %broadcast_in_dim.6), calls=%async_computation | async-start | bytes 4718592 | tf_op jit(solution)/shard_map/all_to_all | solution.py:56
  19.6 0.0 all-gather.3.cloned.1.call-start
  19.6 0.0 copy-done.7
  19.6 0.0 copy-done.8
  19.6 15.3 %all-gather = bf16[16,16,384]{2,1,0:T(8,128)(2,1)S(1)} all-gather(bf16[2,16,384]{2,1,0:T(8,128)(2,1)S(1)} %pad_maximum_fusion), channel_id=2, replica_groups=mesh['depth'=4,'zhi'=4,'core'=2,'zlo'=2,'y'=8] {'zhi','core'}, dimensions={0}, use_global_device_ids=true | all-gather | bytes 221184 | tf_op jit(solution)/shard_map/all_gather | solution.py:73
  34.9 0.0 all-gather.3.cloned.1.call-update
  35.0 0.0 copy-start.1
  35.0 0.0 copy-start.3
  35.0 6.0 %all-to-all-done = bf16[4,96,3072]{2,1,0:T(8,128)(2,1)S(1)} async-done(((bf16[4,96,3072]{2,1,0:T(8,128)(2,1)}), bf16[4,96,3072]{2,1,0:T(8,128)(2,1)S(1)}, u32[]{:S(2)}, u32[]{:S(2)}) %all-to-all-start) | async-done | bytes 2359328 | tf_op jit(solution)/shard_map/all_to_all | solution.py:56
  41.1 1.5 convolution_convert_fusion.3
  42.5 0.0 copy-done.1
  42.5 9.0 %all-to-all-start.1 = ((bf16[16,8,3072]{2,1,0:T(8,128)(2,1)}), bf16[16,8,3072]{2,1,0:T(8,128)(2,1)S(1)}, u32[]{:S(2)}, u32[]{:S(2)}) async-start(bf16[16,8,3072]{2,1,0:T(8,128)(2,1)} %bitcast.21), calls=%async_computation.1 | async-start | bytes 1572864 | tf_op jit(solution)/shard_map/all_to_all | solution.py:56
  51.6 19.8 %all-to-all-done.1 = bf16[16,8,3072]{2,1,0:T(8,128)(2,1)S(1)} async-done(((bf16[16,8,3072]{2,1,0:T(8,128)(2,1)}), bf16[16,8,3072]{2,1,0:T(8,128)(2,1)S(1)}, u32[]{:S(2)}, u32[]{:S(2)}) %all-to-all-start.1) | async-done | bytes 786464 | tf_op jit(solution)/shard_map/all_to_all | solution.py:56
  71.4 0.1 convert_reduce_fusion
  71.5 0.0 copy-start.4
  71.5 0.1 all-gather.3.cloned.1.call-done
  71.6 0.0 copy-done.3
  71.6 2.3 %convolution_convert_fusion.2 = bf16[128,3072]{1,0:T(8,128)(2,1)S(1)} fusion(bf16[384,3072]{1,0:T(8,128)(2,1)} %all-gather.3.cloned.1.call-done, s32[]{:T(128)S(6)} %select_n.6, bf16[128,384]{1,0:T(8,128)(2,1)S(1)} %bitcast.27), kind=kOutput, calls=%fused_computation.2 | convolution fusion | flops 302579712 | bytes 3244036 | tf_op jit(solution)/shard_map/dot_general | solution.py:29
  73.9 0.8 slice.35
  74.7 3.5 %collective-permute-start = (bf16[64,3072]{1,0:T(8,128)(2,1)}, bf16[64,3072]{1,0:T(8,128)(2,1)}, u32[]{:S(2)}, u32[]{:S(2)}) collective-permute-start(bf16[64,3072]{1,0:T(8,128)(2,1)} %slice.35), channel_id=1, source_target_pairs={{0,8},{8,0},{1,9},{9,1},{2,10},{10,2},{3,11},{11,3},{4,12},{12,4},... | collective-permute-start | bytes 1179656 | tf_op jit(solution)/shard_map/ppermute | solution.py:53
  78.3 0.8 broadcast_in_dim.7
  79.1 0.0 copy-done.4
  79.1 6.7 %all-to-all-start.2 = ((bf16[8,8,3072]{2,1,0:T(8,128)(2,1)}), bf16[8,8,3072]{2,1,0:T(8,128)(2,1)S(1)}, u32[]{:S(2)}, u32[]{:S(2)}) async-start(bf16[8,8,3072]{2,1,0:T(8,128)(2,1)} %broadcast_in_dim.7), calls=%async_computation.2 | async-start | bytes 786432 | tf_op jit(solution)/shard_map/all_to_all | solution.py:56
  85.8 1.9 collective-permute-done
  87.7 1.8 add_convert_fusion.1
  89.6 10.6 %all-to-all-done.2 = bf16[8,8,3072]{2,1,0:T(8,128)(2,1)S(1)} async-done(((bf16[8,8,3072]{2,1,0:T(8,128)(2,1)}), bf16[8,8,3072]{2,1,0:T(8,128)(2,1)S(1)}, u32[]{:S(2)}, u32[]{:S(2)}) %all-to-all-start.2) | async-done | bytes 393248 | tf_op jit(solution)/shard_map/all_to_all | solution.py:56
  100.2 3.5 %all-to-all-start.3 = ((bf16[8,8,3072]{2,1,0:T(8,128)(2,1)}), bf16[8,8,3072]{2,1,0:T(8,128)(2,1)S(1)}, u32[]{:S(2)}, u32[]{:S(2)}) async-start(bf16[8,8,3072]{2,1,0:T(8,128)(2,1)} %bitcast.24), calls=%async_computation.3 | async-start | bytes 786432 | tf_op jit(solution)/shard_map/all_to_all | solution.py:56
  103.7 0.0 reduce-scatter.2.cloned.1.call-start
  103.7 2.3 %collective-permute-start.4 = (bf16[64,3072]{1,0:T(8,128)(2,1)S(1)}, bf16[64,3072]{1,0:T(8,128)(2,1)S(1)}, u32[]{:S(2)}, u32[]{:S(2)}) collective-permute-start(bf16[64,3072]{1,0:T(8,128)(2,1)S(1)} %bitcast.22), channel_id=1, source_target_pairs={{0,8},{8,0},{1,9},{9,1},{2,10},{10,2},{3,11},{11,3},{4,12},{12,4},... | collective-permute-start | bytes 1179656 | tf_op jit(solution)/shard_map/ppermute | solution.py:53
  106.0 8.9 %collective-permute-done.4 = bf16[64,3072]{1,0:T(8,128)(2,1)S(1)} collective-permute-done((bf16[64,3072]{1,0:T(8,128)(2,1)S(1)}, bf16[64,3072]{1,0:T(8,128)(2,1)S(1)}, u32[]{:S(2)}, u32[]{:S(2)}) %collective-permute-start.4) | collective-permute-done | bytes 393248 | tf_op jit(solution)/shard_map/ppermute | solution.py:53
  114.9 3.2 %convolution_convert_fusion = bf16[384,3072]{1,0:T(8,128)(2,1)} fusion(bf16[64,3072]{1,0:T(8,128)(2,1)S(1)} %collective-permute-done.4, bf16[64,3072]{1,0:T(8,128)(2,1)S(1)} %bitcast.23, s32[]{:T(128)S(6)} %select_n.6, bf16[128,384]{1,0:T(8,128)(2,1)} %bitcast.28), kind=kOutput, calls=%fused_computation | convolution fusion | flops 304939008 | bytes 3244036 | tf_op jit(solution)/shard_map/dot_general | solution.py:29
  118.0 0.0 copy-start.5
  118.0 0.0 copy-start.2
  118.0 0.0 reduce-scatter.2.cloned.1.call-update
  118.1 0.0 all-to-all-done.3
  118.1 0.1 convert_reduce_fusion.1
  118.1 0.8 copy-done.5
  118.9 0.1 fusion.13
  119.0 1.0 broadcast_in_dim.8
  120.0 6.9 %all-to-all-start.4 = ((bf16[16,8,3072]{2,1,0:T(8,128)(2,1)}), bf16[16,8,3072]{2,1,0:T(8,128)(2,1)S(1)}, u32[]{:S(2)}, u32[]{:S(2)}) async-start(bf16[16,8,3072]{2,1,0:T(8,128)(2,1)} %broadcast_in_dim.8), calls=%async_computation.4 | async-start | bytes 1572864 | tf_op jit(solution)/shard_map/all_to_all | solution.py:56
  126.9 18.7 %all-to-all-done.4 = bf16[16,8,3072]{2,1,0:T(8,128)(2,1)S(1)} async-done(((bf16[16,8,3072]{2,1,0:T(8,128)(2,1)}), bf16[16,8,3072]{2,1,0:T(8,128)(2,1)S(1)}, u32[]{:S(2)}, u32[]{:S(2)}) %all-to-all-start.4) | async-done | bytes 786464 | tf_op jit(solution)/shard_map/all_to_all | solution.py:56
  145.6 0.0 copy-done.2
  145.6 0.9 convolution_convert_fusion.1
  146.5 0.0 copy-start
  146.5 1.3 fusion.22
  147.8 2.4 %collective-permute-start.1 = (bf16[96,3072]{1,0:T(8,128)(2,1)S(1)}, bf16[96,3072]{1,0:T(8,128)(2,1)S(1)}, u32[]{:S(2)}, u32[]{:S(2)}) collective-permute-start(bf16[96,3072]{1,0:T(8,128)(2,1)S(1)} %get-tuple-element.13), channel_id=1, source_target_pairs={{0,128},{128,256},{256,384},{384,0},{1,129},{129,257},{257,385},{3... | collective-permute-start | bytes 1769480 | tf_op jit(solution)/shard_map/ppermute | solution.py:50
  150.2 3.4 %collective-permute-start.3 = (bf16[96,3072]{1,0:T(8,128)(2,1)}, bf16[96,3072]{1,0:T(8,128)(2,1)}, u32[]{:S(2)}, u32[]{:S(2)}) collective-permute-start(bf16[96,3072]{1,0:T(8,128)(2,1)} %get-tuple-element.12), channel_id=1, source_target_pairs={{0,384},{128,0},{256,128},{384,256},{1,385},{129,1},{257,129},{385... | collective-permute-start | bytes 1769480 | tf_op jit(solution)/shard_map/ppermute | solution.py:50
  153.6 4.9 %collective-permute-start.2 = (bf16[96,3072]{1,0:T(8,128)(2,1)}, bf16[96,3072]{1,0:T(8,128)(2,1)}, u32[]{:S(2)}, u32[]{:S(2)}) collective-permute-start(bf16[96,3072]{1,0:T(8,128)(2,1)} %get-tuple-element.11), channel_id=1, source_target_pairs={{0,256},{128,384},{256,0},{384,128},{1,257},{129,385},{257,1},{385... | collective-permute-start | bytes 1769480 | tf_op jit(solution)/shard_map/ppermute | solution.py:50
  158.5 1.5 convolution_convert_fusion.4
  160.0 0.0 copy-done
  160.0 17.8 %collective-permute-done.1 = bf16[96,3072]{1,0:T(8,128)(2,1)S(1)} collective-permute-done((bf16[96,3072]{1,0:T(8,128)(2,1)S(1)}, bf16[96,3072]{1,0:T(8,128)(2,1)S(1)}, u32[]{:S(2)}, u32[]{:S(2)}) %collective-permute-start.1) | collective-permute-done | bytes 589856 | tf_op jit(solution)/shard_map/ppermute | solution.py:50
  177.8 0.0 copy-start.6
  177.8 0.8 copy-done.6
  178.7 3.4 %all-to-all-start.5 = ((bf16[8,16,384]{2,1,0:T(8,128)(2,1)}), bf16[8,16,384]{2,1,0:T(8,128)(2,1)S(1)}, u32[]{:S(2)}, u32[]{:S(2)}) async-start(bf16[8,16,384]{2,1,0:T(8,128)(2,1)} %bitcast.10), calls=%async_computation.5 | async-start | bytes 196608 | tf_op jit(solution)/shard_map/all_to_all | solution.py:56
  182.0 0.0 collective-permute-done.3
  182.1 0.0 collective-permute-done.2
  182.1 2.8 %add_convert_fusion = bf16[96,3072]{1,0:T(8,128)(2,1)} fusion(bf16[96,3072]{1,0:T(8,128)(2,1)} %collective-permute-done.3, bf16[96,3072]{1,0:T(8,128)(2,1)} %collective-permute-done.2, bf16[96,3072]{1,0:T(8,128)(2,1)} %copy-done.6, bf16[384,3072]{1,0:T(8,128)(2,1)} %copy-done), kind=kLoop, calls=%fused_computation.5 | loop fusion | flops 2359296 | bytes 2949120 | tf_op jit(solution)/shard_map/convert_element_type | solution.py:105
  184.8 5.8 %all-to-all-done.5 = bf16[8,16,384]{2,1,0:T(8,128)(2,1)S(1)} async-done(((bf16[8,16,384]{2,1,0:T(8,128)(2,1)}), bf16[8,16,384]{2,1,0:T(8,128)(2,1)S(1)}, u32[]{:S(2)}, u32[]{:S(2)}) %all-to-all-start.5) | async-done | bytes 98336 | tf_op jit(solution)/shard_map/all_to_all | solution.py:56
  190.7 0.6 reduce_sum.32
  191.3 0.0 reduce-scatter.2.cloned.1.call-done
  (3 shorter events, 0.1 us)
Async XLA Ops:
  10.0 9.6 %copy-start.7 = (bf16[16,384]{1,0:T(8,128)(2,1)S(1)}, bf16[16,384]{1,0:T(8,128)(2,1)}, u32[]{:S(2)}) copy-start(bf16[16,384]{1,0:T(8,128)(2,1)} %param.5) | copy-start | bytes 36868
  10.0 9.6 %copy-start.8 = (bf16[16,384]{1,0:T(8,128)(2,1)S(1)}, bf16[16,384]{1,0:T(8,128)(2,1)}, u32[]{:S(2)}) copy-start(bf16[16,384]{1,0:T(8,128)(2,1)} %param.4) | copy-start | bytes 36868
  10.0 31.1 %all-to-all-start = ((bf16[4,96,3072]{2,1,0:T(8,128)(2,1)}), bf16[4,96,3072]{2,1,0:T(8,128)(2,1)S(1)}, u32[]{:S(2)}, u32[]{:S(2)}) async-start(bf16[4,96,3072]{2,1,0:T(8,128)(2,1)} %broadcast_in_dim.6), calls=%async_computation | async-start | bytes 4718592 | tf_op jit(solution)/shard_map/all_to_all | solution.py:56
  19.6 52.0 %all-gather.3.cloned.1.call-start = ((), (), s32[]{:S(2)}) async-start(), calls=%async_computation.7 | async-start | bytes 2949120 | tf_op jit(solution)/shard_map/all_gather | solution.py:78
  35.0 7.5 %copy-start.1 = (bf16[8,1,16,384]{3,2,1,0:T(8,128)(2,1)}, bf16[8,1,16,384]{3,2,1,0:T(8,128)(2,1)S(1)}, u32[]{:S(2)}) copy-start(bf16[8,1,16,384]{3,2,1,0:T(8,128)(2,1)S(1)} %get-tuple-element.15) | copy-start | bytes 294916
  35.0 36.6 %copy-start.3 = (bf16[8,1,16,384]{3,2,1,0:T(8,128)(2,1)}, bf16[8,1,16,384]{3,2,1,0:T(8,128)(2,1)S(1)}, u32[]{:S(2)}) copy-start(bf16[8,1,16,384]{3,2,1,0:T(8,128)(2,1)S(1)} %get-tuple-element.14) | copy-start | bytes 294916
  42.5 28.8 %all-to-all-start.1 = ((bf16[16,8,3072]{2,1,0:T(8,128)(2,1)}), bf16[16,8,3072]{2,1,0:T(8,128)(2,1)S(1)}, u32[]{:S(2)}, u32[]{:S(2)}) async-start(bf16[16,8,3072]{2,1,0:T(8,128)(2,1)} %bitcast.21), calls=%async_computation.1 | async-start | bytes 1572864 | tf_op jit(solution)/shard_map/all_to_all | solution.py:56
  71.5 7.6 %copy-start.4 = (f32[8,3072]{1,0:T(8,128)}, f32[8,3072]{1,0:T(8,128)S(1)}, u32[]{:S(2)}) copy-start(f32[8,3072]{1,0:T(8,128)S(1)} %convert_reduce_fusion) | copy-start | bytes 294916
  74.7 13.1 %collective-permute-start = (bf16[64,3072]{1,0:T(8,128)(2,1)}, bf16[64,3072]{1,0:T(8,128)(2,1)}, u32[]{:S(2)}, u32[]{:S(2)}) collective-permute-start(bf16[64,3072]{1,0:T(8,128)(2,1)} %slice.35), channel_id=1, source_target_pairs={{0,8},{8,0},{1,9},{9,1},{2,10},{10,2},{3,11},{11,3},{4,12},{12,4},... | collective-permute-start | bytes 1179656 | tf_op jit(solution)/shard_map/ppermute | solution.py:53
  79.1 21.1 %all-to-all-start.2 = ((bf16[8,8,3072]{2,1,0:T(8,128)(2,1)}), bf16[8,8,3072]{2,1,0:T(8,128)(2,1)S(1)}, u32[]{:S(2)}, u32[]{:S(2)}) async-start(bf16[8,8,3072]{2,1,0:T(8,128)(2,1)} %broadcast_in_dim.7), calls=%async_computation.2 | async-start | bytes 786432 | tf_op jit(solution)/shard_map/all_to_all | solution.py:56
  100.2 17.9 %all-to-all-start.3 = ((bf16[8,8,3072]{2,1,0:T(8,128)(2,1)}), bf16[8,8,3072]{2,1,0:T(8,128)(2,1)S(1)}, u32[]{:S(2)}, u32[]{:S(2)}) async-start(bf16[8,8,3072]{2,1,0:T(8,128)(2,1)} %bitcast.24), calls=%async_computation.3 | async-start | bytes 786432 | tf_op jit(solution)/shard_map/all_to_all | solution.py:56
  103.7 87.6 %reduce-scatter.2.cloned.1.call-start = ((), (), s32[]{:S(2)}) async-start(), calls=%async_computation.8 | async-start | bytes 2949120 | tf_op jit(solution)/shard_map/reduce_scatter | solution.py:107
  103.7 11.2 %collective-permute-start.4 = (bf16[64,3072]{1,0:T(8,128)(2,1)S(1)}, bf16[64,3072]{1,0:T(8,128)(2,1)S(1)}, u32[]{:S(2)}, u32[]{:S(2)}) collective-permute-start(bf16[64,3072]{1,0:T(8,128)(2,1)S(1)} %bitcast.22), channel_id=1, source_target_pairs={{0,8},{8,0},{1,9},{9,1},{2,10},{10,2},{3,11},{11,3},{4,12},{12,4},... | collective-permute-start | bytes 1179656 | tf_op jit(solution)/shard_map/ppermute | solution.py:53
  118.0 0.9 copy-start.5
  118.0 27.5 %copy-start.2 = (bf16[8,1,16,384]{3,2,1,0:T(8,128)(2,1)S(1)}, bf16[8,1,16,384]{3,2,1,0:T(8,128)(2,1)}, u32[]{:S(2)}) copy-start(bf16[8,1,16,384]{3,2,1,0:T(8,128)(2,1)} %copy-done.1) | copy-start | bytes 294916
  120.0 25.6 %all-to-all-start.4 = ((bf16[16,8,3072]{2,1,0:T(8,128)(2,1)}), bf16[16,8,3072]{2,1,0:T(8,128)(2,1)S(1)}, u32[]{:S(2)}, u32[]{:S(2)}) async-start(bf16[16,8,3072]{2,1,0:T(8,128)(2,1)} %broadcast_in_dim.8), calls=%async_computation.4 | async-start | bytes 1572864 | tf_op jit(solution)/shard_map/all_to_all | solution.py:56
  146.5 13.5 %copy-start = (bf16[384,3072]{1,0:T(8,128)(2,1)}, bf16[384,3072]{1,0:T(8,128)(2,1)S(1)}, u32[]{:S(2)}) copy-start(bf16[384,3072]{1,0:T(8,128)(2,1)S(1)} %convolution_convert_fusion.1) | copy-start | bytes 7077892
  147.8 30.0 %collective-permute-start.1 = (bf16[96,3072]{1,0:T(8,128)(2,1)S(1)}, bf16[96,3072]{1,0:T(8,128)(2,1)S(1)}, u32[]{:S(2)}, u32[]{:S(2)}) collective-permute-start(bf16[96,3072]{1,0:T(8,128)(2,1)S(1)} %get-tuple-element.13), channel_id=1, source_target_pairs={{0,128},{128,256},{256,384},{384,0},{1,129},{129,257},{257,385},{3... | collective-permute-start | bytes 1769480 | tf_op jit(solution)/shard_map/ppermute | solution.py:50
  150.2 31.8 %collective-permute-start.3 = (bf16[96,3072]{1,0:T(8,128)(2,1)}, bf16[96,3072]{1,0:T(8,128)(2,1)}, u32[]{:S(2)}, u32[]{:S(2)}) collective-permute-start(bf16[96,3072]{1,0:T(8,128)(2,1)} %get-tuple-element.12), channel_id=1, source_target_pairs={{0,384},{128,0},{256,128},{384,256},{1,385},{129,1},{257,129},{385... | collective-permute-start | bytes 1769480 | tf_op jit(solution)/shard_map/ppermute | solution.py:50
  153.6 28.4 %collective-permute-start.2 = (bf16[96,3072]{1,0:T(8,128)(2,1)}, bf16[96,3072]{1,0:T(8,128)(2,1)}, u32[]{:S(2)}, u32[]{:S(2)}) collective-permute-start(bf16[96,3072]{1,0:T(8,128)(2,1)} %get-tuple-element.11), channel_id=1, source_target_pairs={{0,256},{128,384},{256,0},{384,128},{1,257},{129,385},{257,1},{385... | collective-permute-start | bytes 1769480 | tf_op jit(solution)/shard_map/ppermute | solution.py:50
  177.8 0.8 copy-start.6
  178.7 12.0 %all-to-all-start.5 = ((bf16[8,16,384]{2,1,0:T(8,128)(2,1)}), bf16[8,16,384]{2,1,0:T(8,128)(2,1)S(1)}, u32[]{:S(2)}, u32[]{:S(2)}) async-start(bf16[8,16,384]{2,1,0:T(8,128)(2,1)} %bitcast.10), calls=%async_computation.5 | async-start | bytes 196608 | tf_op jit(solution)/shard_map/all_to_all | solution.py:56
Sparse Core Ops, SparseCore 0:
  35.1 36.4 all-gather.2
  118.2 39.2 reduce-scatter.1

commit v2 on v1

--- a/solution.py
+++ b/solution.py
@@ -3,6 +3,7 @@
 import jax
 import jax.numpy as jnp
 from jax import lax
+from jax.experimental import pallas as pl
 from jax.sharding import Mesh, PartitionSpec as P
 
 bf16, f32 = jnp.bfloat16, jnp.float32
@@ -21,14 +22,46 @@
     return (value, slope)
 
 
-def after(value, *others):
-    return lax.optimization_barrier((value,) + others)[0]
+def tie(*values):
+    return lax.optimization_barrier(values)
 
 
 def contract(left, right, left_at, right_at):
     return lax.dot_general(
         left, right, (((left_at,), (right_at,)), ((), ())), preferred_element_type=f32
     )
+
+
+TILE = 1024
+
+
+def tiled_call(kernel, left, rights, out_rows, flops):
+    cols = rights[0].shape[1]
+    moved = 2 * cols * (sum(r.shape[0] for r in rights) + sum(out_rows))
+    return pl.pallas_call(
+        kernel,
+        grid=(cols // TILE,),
+        in_specs=[pl.BlockSpec(left.shape, lambda j: (0, 0))]
+        + [pl.BlockSpec((r.shape[0], TILE), lambda j: (0, j)) for r in rights],
+        out_specs=[pl.BlockSpec((n, TILE), lambda j: (0, j)) for n in out_rows],
+        out_shape=[jax.ShapeDtypeStruct((n, cols), bf16) for n in out_rows],
+        cost_estimate=pl.CostEstimate(flops=flops, transcendentals=0, bytes_accessed=moved),
+    )(left, *rights)
+
+
+def matmul_parts(left, rights, out_rows, transposed):
+    count = len(rights)
+
+    def kernel(left_ref, *refs):
+        stacked = jnp.concatenate([ref[...] for ref in refs[:count]], 0)
+        result = contract(left_ref[...], stacked, 0 if transposed else 1, 0).astype(bf16)
+        start = 0
+        for ref in refs[count:]:
+            ref[...] = result[start : start + ref.shape[0]]
+            start += ref.shape[0]
+
+    flops = 2 * left.shape[0] * left.shape[1] * rights[0].shape[1]
+    return tiled_call(kernel, left, rights, out_rows, flops)
 
 
 def body(tokens, grad_out, w_up, w_down):
@@ -71,32 +104,37 @@
 
     up_block = exchange(copies(w_up, n_depth), "depth").reshape(feats, hidden)
     both = lax.all_gather(jnp.stack([tokens, grad_out]), ROW, axis=0)
+    w_down, both = tie(w_down, both)
     x_rows = both[:, 0].reshape(group, feats)
-    dy_rows = rolled(both[:, 1].reshape(group, feats), pair_pos * half, 0)
+    dy_rows = both[:, 1].reshape(group, feats)
     x_rot = rolled(x_rows, depth_pos * narrow, 1)
     dy_rot = rolled(dy_rows, depth_pos * narrow, 1)
-    down_block = lax.all_gather(after(w_down, both), "depth", axis=0, tiled=True)
+    dy_swapped = rolled(dy_rot, pair_pos * half, 0)
 
+    down_near, down_back = from_ahead(w_down, 1), from_ahead(w_down, n_depth - 1)
     pre_part = contract(x_rows, up_block, 1, 0).astype(bf16)
-    sent = pre_part.reshape(2 * n_y, piece, hidden)
-    pre = summed(exchange(sent, COL))
+    got = exchange(pre_part.reshape(2 * n_y, piece, hidden), COL)
+    got, down_near, down_back = tie(got, down_near, down_back)
+    pre = summed(got)
+    cut = narrow // 2
+    far_top = from_ahead(down_near[:cut], 1)
+    far_end = from_ahead(down_back[cut:], n_depth - 1)
+    down_blocks = [w_down, down_near, far_top, far_end, down_back]
     act_value, slope = gelu_parts(pre)
     act_near = exchange(copies(act_value.astype(bf16), n_y), "y").reshape(half, hidden)
-
-    grad_part = contract(dy_rows, after(down_block, pre_part), 1, 0).astype(bf16)
-    grad_other = swap(grad_part[half:])
-    grad_pair = (grad_part[:half].astype(f32) + grad_other.astype(f32)).astype(bf16)
-    grad_pair = after(grad_pair, act_near).reshape(n_y, piece, hidden)
-    act = jnp.concatenate([act_near, swap(act_near)], 0)
-    down_part = contract(dy_rows, act, 0, 0).astype(bf16)
-    act_grad = summed(exchange(grad_pair, "y"))
+    held = tie(act_near, *down_blocks)
+    act_near, down_blocks = held[0], held[1:]
+    (grad_part,) = matmul_parts(dy_rot, down_blocks, [group], False)
+    grad_part, act_far = tie(grad_part, swap(act_near))
+    act_grad = summed(exchange(grad_part.reshape(2 * n_y, piece, hidden), COL))
+    down_parts = matmul_parts(dy_swapped, [act_near, act_far], [narrow] * n_depth, True)
     mine = (act_grad * slope).astype(bf16)
+    held = tie(mine, *down_parts)
+    mine, down_parts = held[0], held[1:]
     hidden_grad = exchange(copies(mine, 2 * n_y), COL).reshape(group, hidden)
 
-    def scatter(part):
-        return [part[:narrow]] + [
-            to_ahead(part[j * narrow : (j + 1) * narrow], j) for j in range(1, n_depth)
-        ]
+    def scatter(parts):
+        return [parts[0]] + [to_ahead(parts[j], j) for j in range(1, n_depth)]
 
     def total(parts):
         acc = parts[0].astype(f32)
@@ -104,10 +142,14 @@
             acc = acc + part.astype(f32)
         return acc.astype(bf16)
 
-    grad_down = lax.psum_scatter(down_part, "depth", scatter_dimension=0, tiled=True)
-    up_terms = scatter(contract(x_rot, hidden_grad, 0, 0).astype(bf16))
+    down_terms = scatter(down_parts)
+    up_parts = matmul_parts(x_rot, [hidden_grad], [narrow] * n_depth, True)
+    held = lax.optimization_barrier(tuple(up_parts) + tuple(down_terms))
+    up_parts, down_terms = held[:n_depth], held[n_depth:]
+    grad_down = total(down_terms)
+    up_terms = scatter(up_parts)
     grad_in_part = contract(hidden_grad, up_block, 1, 1).astype(bf16)
-    grad_in_part = after(grad_in_part, up_terms[1])
+    grad_in_part, up_terms[1] = tie(grad_in_part, up_terms[1])
     got = exchange(grad_in_part.reshape(n_row, own_rows, feats), ROW)
     grad_in = summed(got).astype(bf16)
     grad_up = total(up_terms)

time: 199 us -> 196 us (0.985)
  the two profiles are of different devices: /device:TPU:4 before, /device:TPU:1 now
where the time goes in v2:
time: 196 us; the launch traced here: 194 us
  starting transfers between devices  92.6 us (47%)
  waiting for transfers between devices  48.9 us (25%)
  blocking collectives  20.8 us (11%)
  Pallas kernels  11.7 us (6%)
  other arithmetic  8.18 us (4%)
  local copies, waits for them, and re-layouts  7.27 us (4%)
  matrix products  4.04 us (2%)
    all_to_all x6, starting transfers between devices, exchange(): return lax.all_to_all(array, axis, 0, 0, tiled=True)  52 us
    ppermute x6, starting transfers between devices, to_ahead(): lax.ppermute(array, 'depth', [(i, (i + j) % n_depth) for i in range(n_dep...  23.8 us
    all_gather x1, blocking collectives, body(): both = lax.all_gather(jnp.stack([tokens, grad_out]), ROW, axis=0)  20.8 us
    all_to_all x6, waiting for transfers between devices, exchange(): return lax.all_to_all(array, axis, 0, 0, tiled=True)  18.3 us
    ppermute x6, waiting for transfers between devices, to_ahead(): lax.ppermute(array, 'depth', [(i, (i + j) % n_depth) for i in range(n_dep...  16.5 us
    ppermute x4, starting transfers between devices, from_ahead(): lax.ppermute(array, 'depth', [(i, (i - j) % n_depth) for i in range(n_dep...  13.7 us
    ppermute x4, waiting for transfers between devices, from_ahead(): lax.ppermute(array, 'depth', [(i, (i - j) % n_depth) for i in range(n_dep...  13.3 us
    pallas_call x3, Pallas kernels, tiled_call(): pl.pallas_call(kernel, grid=(cols // TILE,), in_specs=[pl.BlockSpec(left....  11.7 us
  transfers between devices with their start and end apart: 17, of which 15 were waited for; matrix products, arithmetic and copies ran while one was open for 6% of the time, Pallas kernels for 6%

profile of v2, /device:TPU:1, one launch (start us, length us, event | category | flops | bytes accessed | tf_op | source)
XLA Modules:
  0.0 194.3 jit_solution(8469192047958840756)
XLA Ops:
  0.6 2.8 %broadcast_in_dim.6 = bf16[4,96,3072]{2,1,0:T(8,128)(2,1)} broadcast(bf16[96,3072]{1,0:T(8,128)(2,1)} %param.6), dimensions={1,2} | broadcast | bytes 2949120 | tf_op jit(solution)/shard_map/broadcast_in_dim | solution.py:92
  3.4 5.0 %all-to-all-start = ((bf16[4,96,3072]{2,1,0:T(8,128)(2,1)}), bf16[4,96,3072]{2,1,0:T(8,128)(2,1)S(1)}, u32[]{:S(2)}, u32[]{:S(2)}) async-start(bf16[4,96,3072]{2,1,0:T(8,128)(2,1)} %broadcast_in_dim.6), calls=%async_computation | async-start | bytes 4718592 | tf_op jit(solution)/shard_map/all_to_all | solution.py:89
  8.4 0.0 copy-done.8
  8.4 0.0 copy-done.9
  8.4 20.8 %all-gather = bf16[16,16,384]{2,1,0:T(8,128)(2,1)S(1)} all-gather(bf16[2,16,384]{2,1,0:T(8,128)(2,1)S(1)} %pad_maximum_fusion), channel_id=2, replica_groups=mesh['depth'=4,'zhi'=4,'core'=2,'zlo'=2,'y'=8] {'zhi','core'}, dimensions={0}, use_global_device_ids=true | all-gather | bytes 221184 | tf_op jit(solution)/shard_map/all_gather | solution.py:106
  29.2 2.7 %all-to-all-done = bf16[4,96,3072]{2,1,0:T(8,128)(2,1)S(1)} async-done(((bf16[4,96,3072]{2,1,0:T(8,128)(2,1)}), bf16[4,96,3072]{2,1,0:T(8,128)(2,1)S(1)}, u32[]{:S(2)}, u32[]{:S(2)}) %all-to-all-start) | async-done | bytes 2359328 | tf_op jit(solution)/shard_map/all_to_all | solution.py:89
  31.9 1.5 fusion
  33.4 13.4 %all-to-all-start.1 = ((bf16[16,8,3072]{2,1,0:T(8,128)(2,1)}), bf16[16,8,3072]{2,1,0:T(8,128)(2,1)S(1)}, u32[]{:S(2)}, u32[]{:S(2)}) async-start(bf16[16,8,3072]{2,1,0:T(8,128)(2,1)} %fusion), calls=%async_computation.1 | async-start | bytes 1572864 | tf_op jit(solution)/shard_map/all_to_all | solution.py:89
  46.8 2.2 %collective-permute-start.1 = (bf16[96,3072]{1,0:T(8,128)(2,1)}, bf16[96,3072]{1,0:T(8,128)(2,1)S(1)}, u32[]{:S(2)}, u32[]{:S(2)}) collective-permute-start(bf16[96,3072]{1,0:T(8,128)(2,1)} %refs_0_), channel_id=1, source_target_pairs={{0,128},{128,256},{256,384},{384,0},{1,129},{129,257},{257,385},{3... | collective-permute-start | bytes 1769480 | tf_op jit(solution)/shard_map/ppermute | solution.py:80
  49.0 4.3 %collective-permute-start = (bf16[96,3072]{1,0:T(8,128)(2,1)}, bf16[96,3072]{1,0:T(8,128)(2,1)}, u32[]{:S(2)}, u32[]{:S(2)}) collective-permute-start(bf16[96,3072]{1,0:T(8,128)(2,1)} %refs_0_), channel_id=1, source_target_pairs={{0,384},{128,0},{256,128},{384,256},{1,385},{129,1},{257,129},{385... | collective-permute-start | bytes 1769480 | tf_op jit(solution)/shard_map/ppermute | solution.py:80
  53.3 9.5 %collective-permute-done.1.refs_4_ = bf16[96,3072]{1,0:T(8,128)(2,1)S(1)} collective-permute-done((bf16[96,3072]{1,0:T(8,128)(2,1)}, bf16[96,3072]{1,0:T(8,128)(2,1)S(1)}, u32[]{:S(2)}, u32[]{:S(2)}) %collective-permute-start.1) | collective-permute-done | bytes 589856 | tf_op jit(solution)/shard_map/ppermute | solution.py:80
  62.8 0.8 copy-done.1
  63.6 0.2 collective-permute-done.refs_1_
  63.8 0.8 all-to-all-done.1
  64.7 0.1 convert_reduce_fusion.1
  64.8 0.0 copy-start.2
  64.8 0.8 broadcast_in_dim.7
  65.6 5.5 %all-to-all-start.2 = ((bf16[8,8,3072]{2,1,0:T(8,128)(2,1)}), bf16[8,8,3072]{2,1,0:T(8,128)(2,1)}, u32[]{:S(2)}, u32[]{:S(2)}) async-start(bf16[8,8,3072]{2,1,0:T(8,128)(2,1)} %broadcast_in_dim.7), calls=%async_computation.2 | async-start | bytes 786432 | tf_op jit(solution)/shard_map/all_to_all | solution.py:89
  71.1 1.0 slice.14
  72.1 0.0 copy-done.2
  72.1 2.2 %collective-permute-start.3 = (bf16[48,3072]{1,0:T(8,128)(2,1)S(1)}, bf16[48,3072]{1,0:T(8,128)(2,1)S(1)}, u32[]{:S(2)}, u32[]{:S(2)}) collective-permute-start(bf16[48,3072]{1,0:T(8,128)(2,1)S(1)} %slice.15), channel_id=1, source_target_pairs={{0,128},{128,256},{256,384},{384,0},{1,129},{129,257},{257,385},{3... | collective-permute-start | bytes 884744 | tf_op jit(solution)/shard_map/ppermute | solution.py:80
  74.3 5.0 %collective-permute-start.2 = (bf16[48,3072]{1,0:T(8,128)(2,1)S(1)}, bf16[48,3072]{1,0:T(8,128)(2,1)S(1)}, u32[]{:S(2)}, u32[]{:S(2)}) collective-permute-start(bf16[48,3072]{1,0:T(8,128)(2,1)S(1)} %slice.14), channel_id=1, source_target_pairs={{0,384},{128,0},{256,128},{384,256},{1,385},{129,1},{257,129},{385... | collective-permute-start | bytes 884744 | tf_op jit(solution)/shard_map/ppermute | solution.py:80
  79.3 2.6 %collective-permute-done.3.refs_3_ = bf16[48,3072]{1,0:T(8,128)(2,1)S(1)} collective-permute-done((bf16[48,3072]{1,0:T(8,128)(2,1)S(1)}, bf16[48,3072]{1,0:T(8,128)(2,1)S(1)}, u32[]{:S(2)}, u32[]{:S(2)}) %collective-permute-start.3) | collective-permute-done | bytes 294944 | tf_op jit(solution)/shard_map/ppermute | solution.py:80
  81.9 1.1 collective-permute-done.2.refs_2_
  83.0 0.0 all-to-all-done.2
  83.0 3.1 %collective-permute-start.4 = (bf16[64,3072]{1,0:T(8,128)(2,1)}, bf16[64,3072]{1,0:T(8,128)(2,1)}, u32[]{:S(2)}, u32[]{:S(2)}) collective-permute-start(bf16[64,3072]{1,0:T(8,128)(2,1)} %bitcast.7.refs_0_), channel_id=1, source_target_pairs={{0,8},{8,0},{1,9},{9,1},{2,10},{10,2},{3,11},{11,3},{4,12},{12,4},... | collective-permute-start | bytes 1179656 | tf_op jit(solution)/shard_map/ppermute | solution.py:86
  86.1 0.8 fusion.12.left_ref
  86.9 0.0 copy-done.6
  86.9 0.0 copy-done.7
  86.9 4.1 %shard_map.67 = bf16[128,3072]{1,0:T(8,128)(2,1)} custom-call(bf16[128,384]{1,0:T(8,128)(2,1)} %fusion.12.left_ref, bf16[96,3072]{1,0:T(8,128)(2,1)} %refs_0_, bf16[96,3072]{1,0:T(8,128)(2,1)} %collective-permute-done.refs_1_, bf16[48,3072]{1,0:T(8,128)(2,1)} %copy-done.7, bf16[48,3072]{1,0:T(8,128)(2,1)} %copy-done.6, bf16[96,3072]{1,0:T(8,128)(2,1)} %copy-done.1), custom_call_target="tpu_custom_call" | custom-call | flops 301989888 | bytes 3145728 | tf_op jit(solution)/shard_map/pallas_call | solution.py:41
  91.0 0.8 collective-permute-done.4.refs_1_
  91.8 7.7 %all-to-all-start.3 = ((bf16[16,8,3072]{2,1,0:T(8,128)(2,1)}), bf16[16,8,3072]{2,1,0:T(8,128)(2,1)S(1)}, u32[]{:S(2)}, u32[]{:S(2)}) async-start(bf16[16,8,3072]{2,1,0:T(8,128)(2,1)} %bitcast.20), calls=%async_computation.3 | async-start | bytes 1572864 | tf_op jit(solution)/shard_map/all_to_all | solution.py:89
  99.5 0.0 copy-done.3
  99.5 0.8 fusion.11.left_ref
  100.2 3.8 %shard_map.68 = (bf16[96,3072]{1,0:T(8,128)(2,1)}, bf16[96,3072]{1,0:T(8,128)(2,1)}, bf16[96,3072]{1,0:T(8,128)(2,1)}, bf16[96,3072]{1,0:T(8,128)(2,1)}) custom-call(bf16[128,384]{1,0:T(8,128)(2,1)} %fusion.11.left_ref, bf16[64,3072]{1,0:T(8,128)(2,1)} %bitcast.7.refs_0_, bf16[64,3072]{1,0:T(8,128)(2,1)} %collective-permute-done.4.refs_1_), custom_call_target="tpu_custom_call" | custom-call | flops 301989888 | bytes 3145728 | tf_op jit(solution)/shard_map/pallas_call | solution.py:41
  104.0 8.7 %all-to-all-done.3 = bf16[16,8,3072]{2,1,0:T(8,128)(2,1)S(1)} async-done(((bf16[16,8,3072]{2,1,0:T(8,128)(2,1)}), bf16[16,8,3072]{2,1,0:T(8,128)(2,1)S(1)}, u32[]{:S(2)}, u32[]{:S(2)}) %all-to-all-start.3) | async-done | bytes 786464 | tf_op jit(solution)/shard_map/all_to_all | solution.py:89
  112.8 0.1 convert_reduce_fusion
  112.9 0.1 fusion.9
  113.0 1.0 broadcast_in_dim.8
  113.9 8.8 %all-to-all-start.4 = ((bf16[16,8,3072]{2,1,0:T(8,128)(2,1)}), bf16[16,8,3072]{2,1,0:T(8,128)(2,1)S(1)}, u32[]{:S(2)}, u32[]{:S(2)}) async-start(bf16[16,8,3072]{2,1,0:T(8,128)(2,1)} %broadcast_in_dim.8), calls=%async_computation.4 | async-start | bytes 1572864 | tf_op jit(solution)/shard_map/all_to_all | solution.py:89
  122.8 3.3 %collective-permute-start.5 = (bf16[96,3072]{1,0:T(8,128)(2,1)}, bf16[96,3072]{1,0:T(8,128)(2,1)}, u32[]{:S(2)}, u32[]{:S(2)}) collective-permute-start(bf16[96,3072]{1,0:T(8,128)(2,1)} %get-tuple-element.62), channel_id=1, source_target_pairs={{0,128},{128,256},{256,384},{384,0},{1,129},{129,257},{257,385},{3... | collective-permute-start | bytes 1769480 | tf_op jit(solution)/shard_map/ppermute | solution.py:83
  126.0 4.9 %collective-permute-start.6 = (bf16[96,3072]{1,0:T(8,128)(2,1)}, bf16[96,3072]{1,0:T(8,128)(2,1)}, u32[]{:S(2)}, u32[]{:S(2)}) collective-permute-start(bf16[96,3072]{1,0:T(8,128)(2,1)} %get-tuple-element.63), channel_id=1, source_target_pairs={{0,256},{128,384},{256,0},{384,128},{1,257},{129,385},{257,1},{385... | collective-permute-start | bytes 1769480 | tf_op jit(solution)/shard_map/ppermute | solution.py:83
  130.9 3.1 %collective-permute-start.7 = (bf16[96,3072]{1,0:T(8,128)(2,1)}, bf16[96,3072]{1,0:T(8,128)(2,1)}, u32[]{:S(2)}, u32[]{:S(2)}) collective-permute-start(bf16[96,3072]{1,0:T(8,128)(2,1)} %get-tuple-element.64), channel_id=1, source_target_pairs={{0,384},{128,0},{256,128},{384,256},{1,385},{129,1},{257,129},{385... | collective-permute-start | bytes 1769480 | tf_op jit(solution)/shard_map/ppermute | solution.py:83
  134.0 0.8 fusion.10.left_ref
  134.7 3.6 %all-to-all-done.4 = bf16[16,8,3072]{2,1,0:T(8,128)(2,1)S(1)} async-done(((bf16[16,8,3072]{2,1,0:T(8,128)(2,1)}), bf16[16,8,3072]{2,1,0:T(8,128)(2,1)S(1)}, u32[]{:S(2)}, u32[]{:S(2)}) %all-to-all-start.4) | async-done | bytes 786464 | tf_op jit(solution)/shard_map/all_to_all | solution.py:89
  138.3 0.9 copy-done
  139.2 3.7 %shard_map.69 = (bf16[96,3072]{1,0:T(8,128)(2,1)}, bf16[96,3072]{1,0:T(8,128)(2,1)}, bf16[96,3072]{1,0:T(8,128)(2,1)}, bf16[96,3072]{1,0:T(8,128)(2,1)}) custom-call(bf16[128,384]{1,0:T(8,128)(2,1)} %fusion.10.left_ref, bf16[128,3072]{1,0:T(8,128)(2,1)} %bitcast.19), custom_call_target="tpu_custom_call" | custom-call | flops 301989888 | bytes 3145728 | tf_op jit(solution)/shard_map/pallas_call | solution.py:41
  142.9 0.0 collective-permute-done.5
  143.0 7.6 %collective-permute-done.6 = bf16[96,3072]{1,0:T(8,128)(2,1)} collective-permute-done((bf16[96,3072]{1,0:T(8,128)(2,1)}, bf16[96,3072]{1,0:T(8,128)(2,1)}, u32[]{:S(2)}, u32[]{:S(2)}) %collective-permute-start.6) | collective-permute-done | bytes 589856 | tf_op jit(solution)/shard_map/ppermute | solution.py:83
  150.6 4.3 %collective-permute-done.7 = bf16[96,3072]{1,0:T(8,128)(2,1)} collective-permute-done((bf16[96,3072]{1,0:T(8,128)(2,1)}, bf16[96,3072]{1,0:T(8,128)(2,1)}, u32[]{:S(2)}, u32[]{:S(2)}) %collective-permute-start.7) | collective-permute-done | bytes 589856 | tf_op jit(solution)/shard_map/ppermute | solution.py:83
  154.9 6.4 %collective-permute-start.8 = (bf16[96,3072]{1,0:T(8,128)(2,1)}, bf16[96,3072]{1,0:T(8,128)(2,1)S(1)}, u32[]{:S(2)}, u32[]{:S(2)}) collective-permute-start(bf16[96,3072]{1,0:T(8,128)(2,1)} %get-tuple-element.65), channel_id=1, source_target_pairs={{0,128},{128,256},{256,384},{384,0},{1,129},{129,257},{257,385},{3... | collective-permute-start | bytes 1769480 | tf_op jit(solution)/shard_map/ppermute | solution.py:83
  161.4 2.1 %collective-permute-start.9 = (bf16[96,3072]{1,0:T(8,128)(2,1)}, bf16[96,3072]{1,0:T(8,128)(2,1)S(1)}, u32[]{:S(2)}, u32[]{:S(2)}) collective-permute-start(bf16[96,3072]{1,0:T(8,128)(2,1)} %get-tuple-element.69), channel_id=1, source_target_pairs={{0,256},{128,384},{256,0},{384,128},{1,257},{129,385},{257,1},{385... | collective-permute-start | bytes 1769480 | tf_op jit(solution)/shard_map/ppermute | solution.py:83
  163.5 4.1 %collective-permute-start.10 = (bf16[96,3072]{1,0:T(8,128)(2,1)}, bf16[96,3072]{1,0:T(8,128)(2,1)}, u32[]{:S(2)}, u32[]{:S(2)}) collective-permute-start(bf16[96,3072]{1,0:T(8,128)(2,1)} %get-tuple-element.70), channel_id=1, source_target_pairs={{0,384},{128,0},{256,128},{384,256},{1,385},{129,1},{257,129},{385... | collective-permute-start | bytes 1769480 | tf_op jit(solution)/shard_map/ppermute | solution.py:83
  167.6 2.6 %convolution_convert_fusion.1 = bf16[128,384]{1,0:T(8,128)(2,1)} fusion(bf16[384,3072]{1,0:T(8,128)(2,1)S(1)} %bitcast.18, bf16[16,8,3072]{2,1,0:T(8,128)(2,1)} %copy-done), kind=kOutput, calls=%fused_computation.6 | convolution fusion | flops 302039040 | bytes 3244032 | tf_op jit(solution)/shard_map/dot_general | solution.py:30
  170.2 0.0 copy-done.4
  170.2 2.6 %add_convert_fusion = bf16[96,3072]{1,0:T(8,128)(2,1)} fusion(bf16[96,3072]{1,0:T(8,128)(2,1)} %collective-permute-done.7, bf16[96,3072]{1,0:T(8,128)(2,1)} %collective-permute-done.6, bf16[96,3072]{1,0:T(8,128)(2,1)} %collective-permute-done.5, bf16[96,3072]{1,0:T(8,128)(2,1)S(1)} %copy-done.4), kind=kLoop, calls=%fused_computation.4 | loop fusion | flops 2359296 | bytes 2949120 | tf_op jit(solution)/shard_map/convert_element_type | solution.py:143
  172.8 1.0 collective-permute-done.8
  173.9 11.7 %all-to-all-start.5 = ((bf16[8,16,384]{2,1,0:T(8,128)(2,1)}), bf16[8,16,384]{2,1,0:T(8,128)(2,1)S(1)}, u32[]{:S(2)}, u32[]{:S(2)}) async-start(bf16[8,16,384]{2,1,0:T(8,128)(2,1)} %bitcast.10), calls=%async_computation.5 | async-start | bytes 196608 | tf_op jit(solution)/shard_map/all_to_all | solution.py:89
  185.5 1.0 collective-permute-done.9
  186.5 2.5 %collective-permute-done.10 = bf16[96,3072]{1,0:T(8,128)(2,1)} collective-permute-done((bf16[96,3072]{1,0:T(8,128)(2,1)}, bf16[96,3072]{1,0:T(8,128)(2,1)}, u32[]{:S(2)}, u32[]{:S(2)}) %collective-permute-start.10) | collective-permute-done | bytes 589856 | tf_op jit(solution)/shard_map/ppermute | solution.py:83
  189.0 0.0 copy-done.5
  189.0 2.2 %add_convert_fusion.1 = bf16[96,3072]{1,0:T(8,128)(2,1)} fusion(bf16[96,3072]{1,0:T(8,128)(2,1)} %collective-permute-done.10, bf16[96,3072]{1,0:T(8,128)(2,1)S(1)} %collective-permute-done.9, bf16[96,3072]{1,0:T(8,128)(2,1)S(1)} %collective-permute-done.8, bf16[96,3072]{1,0:T(8,128)(2,1)S(1)} %copy-done.5), kind=kLoop, calls=%fused_computation.5 | loop fusion | flops 2359296 | bytes 2949120 | tf_op jit(solution)/shard_map/convert_element_type | solution.py:143
  191.2 2.4 %all-to-all-done.5 = bf16[8,16,384]{2,1,0:T(8,128)(2,1)S(1)} async-done(((bf16[8,16,384]{2,1,0:T(8,128)(2,1)}), bf16[8,16,384]{2,1,0:T(8,128)(2,1)S(1)}, u32[]{:S(2)}, u32[]{:S(2)}) %all-to-all-start.5) | async-done | bytes 98336 | tf_op jit(solution)/shard_map/all_to_all | solution.py:89
  193.7 0.6 reduce_sum.32
  (13 shorter events, 0.1 us)
Async XLA Ops:
  3.4 5.0 %copy-start.8 = (bf16[16,384]{1,0:T(8,128)(2,1)S(1)}, bf16[16,384]{1,0:T(8,128)(2,1)}, u32[]{:S(2)}) copy-start(bf16[16,384]{1,0:T(8,128)(2,1)} %param.5) | copy-start | bytes 36868
  3.4 5.0 %copy-start.9 = (bf16[16,384]{1,0:T(8,128)(2,1)S(1)}, bf16[16,384]{1,0:T(8,128)(2,1)}, u32[]{:S(2)}) copy-start(bf16[16,384]{1,0:T(8,128)(2,1)} %param.4) | copy-start | bytes 36868
  3.4 28.5 %all-to-all-start = ((bf16[4,96,3072]{2,1,0:T(8,128)(2,1)}), bf16[4,96,3072]{2,1,0:T(8,128)(2,1)S(1)}, u32[]{:S(2)}, u32[]{:S(2)}) async-start(bf16[4,96,3072]{2,1,0:T(8,128)(2,1)} %broadcast_in_dim.6), calls=%async_computation | async-start | bytes 4718592 | tf_op jit(solution)/shard_map/all_to_all | solution.py:89
  33.4 31.3 %all-to-all-start.1 = ((bf16[16,8,3072]{2,1,0:T(8,128)(2,1)}), bf16[16,8,3072]{2,1,0:T(8,128)(2,1)S(1)}, u32[]{:S(2)}, u32[]{:S(2)}) async-start(bf16[16,8,3072]{2,1,0:T(8,128)(2,1)} %fusion), calls=%async_computation.1 | async-start | bytes 1572864 | tf_op jit(solution)/shard_map/all_to_all | solution.py:89
  46.8 16.0 %collective-permute-start.1 = (bf16[96,3072]{1,0:T(8,128)(2,1)}, bf16[96,3072]{1,0:T(8,128)(2,1)S(1)}, u32[]{:S(2)}, u32[]{:S(2)}) collective-permute-start(bf16[96,3072]{1,0:T(8,128)(2,1)} %refs_0_), channel_id=1, source_target_pairs={{0,128},{128,256},{256,384},{384,0},{1,129},{129,257},{257,385},{3... | collective-permute-start | bytes 1769480 | tf_op jit(solution)/shard_map/ppermute | solution.py:80
  49.0 14.8 %collective-permute-start = (bf16[96,3072]{1,0:T(8,128)(2,1)}, bf16[96,3072]{1,0:T(8,128)(2,1)}, u32[]{:S(2)}, u32[]{:S(2)}) collective-permute-start(bf16[96,3072]{1,0:T(8,128)(2,1)} %refs_0_), channel_id=1, source_target_pairs={{0,384},{128,0},{256,128},{384,256},{1,385},{129,1},{257,129},{385... | collective-permute-start | bytes 1769480 | tf_op jit(solution)/shard_map/ppermute | solution.py:80
  62.8 0.8 copy-start.1
  64.8 7.3 %copy-start.2 = (bf16[96,3072]{1,0:T(8,128)(2,1)S(1)}, bf16[96,3072]{1,0:T(8,128)(2,1)}, u32[]{:S(2)}) copy-start(bf16[96,3072]{1,0:T(8,128)(2,1)} %copy-done.1) | copy-start | bytes 1769476
  65.6 17.4 %all-to-all-start.2 = ((bf16[8,8,3072]{2,1,0:T(8,128)(2,1)}), bf16[8,8,3072]{2,1,0:T(8,128)(2,1)}, u32[]{:S(2)}, u32[]{:S(2)}) async-start(bf16[8,8,3072]{2,1,0:T(8,128)(2,1)} %broadcast_in_dim.7), calls=%async_computation.2 | async-start | bytes 786432 | tf_op jit(solution)/shard_map/all_to_all | solution.py:89
  72.1 9.8 %collective-permute-start.3 = (bf16[48,3072]{1,0:T(8,128)(2,1)S(1)}, bf16[48,3072]{1,0:T(8,128)(2,1)S(1)}, u32[]{:S(2)}, u32[]{:S(2)}) collective-permute-start(bf16[48,3072]{1,0:T(8,128)(2,1)S(1)} %slice.15), channel_id=1, source_target_pairs={{0,128},{128,256},{256,384},{384,0},{1,129},{129,257},{257,385},{3... | collective-permute-start | bytes 884744 | tf_op jit(solution)/shard_map/ppermute | solution.py:80
  74.3 8.6 %collective-permute-start.2 = (bf16[48,3072]{1,0:T(8,128)(2,1)S(1)}, bf16[48,3072]{1,0:T(8,128)(2,1)S(1)}, u32[]{:S(2)}, u32[]{:S(2)}) collective-permute-start(bf16[48,3072]{1,0:T(8,128)(2,1)S(1)} %slice.14), channel_id=1, source_target_pairs={{0,384},{128,0},{256,128},{384,256},{1,385},{129,1},{257,129},{385... | collective-permute-start | bytes 884744 | tf_op jit(solution)/shard_map/ppermute | solution.py:80
  81.9 5.0 %copy-start.6 = (bf16[48,3072]{1,0:T(8,128)(2,1)}, bf16[48,3072]{1,0:T(8,128)(2,1)S(1)}, u32[]{:S(2)}) copy-start(bf16[48,3072]{1,0:T(8,128)(2,1)S(1)} %collective-permute-done.3.refs_3_) | copy-start | bytes 884740
  83.0 3.9 %copy-start.7 = (bf16[48,3072]{1,0:T(8,128)(2,1)}, bf16[48,3072]{1,0:T(8,128)(2,1)S(1)}, u32[]{:S(2)}) copy-start(bf16[48,3072]{1,0:T(8,128)(2,1)S(1)} %collective-permute-done.2.refs_2_) | copy-start | bytes 884740
  83.0 8.8 %collective-permute-start.4 = (bf16[64,3072]{1,0:T(8,128)(2,1)}, bf16[64,3072]{1,0:T(8,128)(2,1)}, u32[]{:S(2)}, u32[]{:S(2)}) collective-permute-start(bf16[64,3072]{1,0:T(8,128)(2,1)} %bitcast.7.refs_0_), channel_id=1, source_target_pairs={{0,8},{8,0},{1,9},{9,1},{2,10},{10,2},{3,11},{11,3},{4,12},{12,4},... | collective-permute-start | bytes 1179656 | tf_op jit(solution)/shard_map/ppermute | solution.py:86
  91.0 8.5 %copy-start.3 = (bf16[128,384]{1,0:T(8,128)(2,1)S(1)}, bf16[128,384]{1,0:T(8,128)(2,1)}, u32[]{:S(2)}) copy-start(bf16[128,384]{1,0:T(8,128)(2,1)} %fusion.12.left_ref) | copy-start | bytes 294916
  91.8 21.0 %all-to-all-start.3 = ((bf16[16,8,3072]{2,1,0:T(8,128)(2,1)}), bf16[16,8,3072]{2,1,0:T(8,128)(2,1)S(1)}, u32[]{:S(2)}, u32[]{:S(2)}) async-start(bf16[16,8,3072]{2,1,0:T(8,128)(2,1)} %bitcast.20), calls=%async_computation.3 | async-start | bytes 1572864 | tf_op jit(solution)/shard_map/all_to_all | solution.py:89
  113.9 24.4 %all-to-all-start.4 = ((bf16[16,8,3072]{2,1,0:T(8,128)(2,1)}), bf16[16,8,3072]{2,1,0:T(8,128)(2,1)S(1)}, u32[]{:S(2)}, u32[]{:S(2)}) async-start(bf16[16,8,3072]{2,1,0:T(8,128)(2,1)} %broadcast_in_dim.8), calls=%async_computation.4 | async-start | bytes 1572864 | tf_op jit(solution)/shard_map/all_to_all | solution.py:89
  122.8 20.2 %collective-permute-start.5 = (bf16[96,3072]{1,0:T(8,128)(2,1)}, bf16[96,3072]{1,0:T(8,128)(2,1)}, u32[]{:S(2)}, u32[]{:S(2)}) collective-permute-start(bf16[96,3072]{1,0:T(8,128)(2,1)} %get-tuple-element.62), channel_id=1, source_target_pairs={{0,128},{128,256},{256,384},{384,0},{1,129},{129,257},{257,385},{3... | collective-permute-start | bytes 1769480 | tf_op jit(solution)/shard_map/ppermute | solution.py:83
  126.0 24.6 %collective-permute-start.6 = (bf16[96,3072]{1,0:T(8,128)(2,1)}, bf16[96,3072]{1,0:T(8,128)(2,1)}, u32[]{:S(2)}, u32[]{:S(2)}) collective-permute-start(bf16[96,3072]{1,0:T(8,128)(2,1)} %get-tuple-element.63), channel_id=1, source_target_pairs={{0,256},{128,384},{256,0},{384,128},{1,257},{129,385},{257,1},{385... | collective-permute-start | bytes 1769480 | tf_op jit(solution)/shard_map/ppermute | solution.py:83
  130.9 24.0 %collective-permute-start.7 = (bf16[96,3072]{1,0:T(8,128)(2,1)}, bf16[96,3072]{1,0:T(8,128)(2,1)}, u32[]{:S(2)}, u32[]{:S(2)}) collective-permute-start(bf16[96,3072]{1,0:T(8,128)(2,1)} %get-tuple-element.64), channel_id=1, source_target_pairs={{0,384},{128,0},{256,128},{384,256},{1,385},{129,1},{257,129},{385... | collective-permute-start | bytes 1769480 | tf_op jit(solution)/shard_map/ppermute | solution.py:83
  138.3 0.9 copy-start
  154.9 15.3 %copy-start.4 = (bf16[96,3072]{1,0:T(8,128)(2,1)S(1)}, bf16[96,3072]{1,0:T(8,128)(2,1)}, u32[]{:S(2)}) copy-start(bf16[96,3072]{1,0:T(8,128)(2,1)} %get-tuple-element.71) | copy-start | bytes 1769476
  154.9 18.9 %collective-permute-start.8 = (bf16[96,3072]{1,0:T(8,128)(2,1)}, bf16[96,3072]{1,0:T(8,128)(2,1)S(1)}, u32[]{:S(2)}, u32[]{:S(2)}) collective-permute-start(bf16[96,3072]{1,0:T(8,128)(2,1)} %get-tuple-element.65), channel_id=1, source_target_pairs={{0,128},{128,256},{256,384},{384,0},{1,129},{129,257},{257,385},{3... | collective-permute-start | bytes 1769480 | tf_op jit(solution)/shard_map/ppermute | solution.py:83
  161.4 25.1 %collective-permute-start.9 = (bf16[96,3072]{1,0:T(8,128)(2,1)}, bf16[96,3072]{1,0:T(8,128)(2,1)S(1)}, u32[]{:S(2)}, u32[]{:S(2)}) collective-permute-start(bf16[96,3072]{1,0:T(8,128)(2,1)} %get-tuple-element.69), channel_id=1, source_target_pairs={{0,256},{128,384},{256,0},{384,128},{1,257},{129,385},{257,1},{385... | collective-permute-start | bytes 1769480 | tf_op jit(solution)/shard_map/ppermute | solution.py:83
  163.5 25.5 %collective-permute-start.10 = (bf16[96,3072]{1,0:T(8,128)(2,1)}, bf16[96,3072]{1,0:T(8,128)(2,1)}, u32[]{:S(2)}, u32[]{:S(2)}) collective-permute-start(bf16[96,3072]{1,0:T(8,128)(2,1)} %get-tuple-element.70), channel_id=1, source_target_pairs={{0,384},{128,0},{256,128},{384,256},{1,385},{129,1},{257,129},{385... | collective-permute-start | bytes 1769480 | tf_op jit(solution)/shard_map/ppermute | solution.py:83
  170.2 18.8 %copy-start.5 = (bf16[96,3072]{1,0:T(8,128)(2,1)S(1)}, bf16[96,3072]{1,0:T(8,128)(2,1)}, u32[]{:S(2)}) copy-start(bf16[96,3072]{1,0:T(8,128)(2,1)} %get-tuple-element.67) | copy-start | bytes 1769476
  173.9 19.8 %all-to-all-start.5 = ((bf16[8,16,384]{2,1,0:T(8,128)(2,1)}), bf16[8,16,384]{2,1,0:T(8,128)(2,1)S(1)}, u32[]{:S(2)}, u32[]{:S(2)}) async-start(bf16[8,16,384]{2,1,0:T(8,128)(2,1)} %bitcast.10), calls=%async_computation.5 | async-start | bytes 196608 | tf_op jit(solution)/shard_map/all_to_all | solution.py:89
